TPU v7x, 512 devices: a whole 4x4x16 slice. The times are simulated.
512 devices in a mesh: flux: 16 (over z), obs: 32 (over y, x, core).
Axes of the slice: x: 4, y: 4, z: 16, core: 2. Of those that a mesh axis runs over, the one named last changes fastest.
Arguments:
- footprint: bfloat16 [4096, 4, 4, 2, 4096], P(('flux', 'obs')), may hold values from 0.00049972534 to 0.049804688
- obs_hour: int32 [4096, 4], P(('flux', 'obs')), may hold values from 0 to 3
- tile_list: int32 [4096, 4], P(('flux', 'obs')), may hold values from 0 to 511, as said below
- tile_row: int32 [512], replicated, may hold values from 0 to 511, as said below
- flux: bfloat16 [512, 5, 4096], P('flux'), may hold values from -6 to 6
- observed: float32 [4096, 4], P(('flux', 'obs')), may hold values from -18 to 18
- obs_var: float32 [4096, 4], P(('flux', 'obs')), may hold values from 0.5 to 4
Outputs:
- modeled: float32 [4096, 4], P(('flux', 'obs'))
- gradient: float32 [512, 5, 4096], P('flux', None, 'obs')
Inputs may be any that keep to these rules, and one draw needn't show every extreme that they name: `tile_row`: A permutation: every tile has its own storage row, and the row r lies on index r // 32 of flux. `tile_list`: among the 32 listed tiles of one device's 8 blocks, at most 4 have storage rows on one index of flux; on every device some index of flux gets exactly 4.
All inputs are finite; a program needn't handle non-finite values.
Results may differ from a plain program's by a relative error of at most 0.0019.
Values may be sent and summed in bfloat16 or wider, within the bound.
A program may use at most 64 MiB of HBM per device.

v0:
```python
import jax
import jax.numpy as jnp
from jax import lax
from jax.sharding import PartitionSpec as P


def shards(footprint, obs_hour, tile_list, tile_row, flux, observed, obs_var):
    columns = lax.axis_size("obs")
    block_count, slot_width, sounding_count, lag_count, cell_count = footprint.shape
    tile_count, hour_count, _ = flux.shape
    chunk = cell_count // columns
    me = lax.axis_index("obs")
    table_hits = tile_list[..., None] == jnp.arange(tile_row.shape[0], dtype=jnp.int32)
    storage = jnp.sum(jnp.where(table_hits, tile_row, 0), axis=-1)
    numbers = jnp.concatenate(
        [storage.astype(jnp.float32), obs_hour.astype(jnp.float32), observed, obs_var], axis=1
    )
    numbers = lax.all_gather(numbers, "obs", axis=0, tiled=True)
    rows = numbers[:, 0:4].astype(jnp.int32)
    hours = numbers[:, 4:8].astype(jnp.int32)
    own_flux = lax.dynamic_slice_in_dim(flux, me * chunk, chunk, axis=2)
    all_flux = lax.all_gather(own_flux, "flux", axis=0, tiled=True)
    total = all_flux.shape[0]
    feet = footprint.reshape(-1, columns, chunk).transpose(1, 0, 2)
    feet = lax.all_to_all(feet, "obs", split_axis=0, concat_axis=0, tiled=True)
    blocks = block_count * columns
    feet = feet.reshape(blocks, slot_width, sounding_count, lag_count, chunk)
    onehot = rows.reshape(-1)[:, None] == jnp.arange(total, dtype=jnp.int32)[None, :]
    windows = jnp.dot(
        onehot.astype(jnp.bfloat16),
        all_flux.reshape(total, hour_count * chunk),
        preferred_element_type=jnp.float32,
    ).reshape(blocks, slot_width, hour_count, chunk)
    hour_at = hours[:, :, None] + jnp.arange(lag_count, dtype=jnp.int32)
    select = hour_at[..., None] == jnp.arange(hour_count, dtype=jnp.int32)
    picked = 0.0
    for h in range(hour_count):
        picked = picked + jnp.where(
            select[:, None, :, :, h, None], windows[:, :, None, None, h, :], 0.0
        )
    partial_value = jnp.sum(feet.astype(jnp.float32) * picked, axis=(1, 3, 4))
    modeled_all = lax.psum(partial_value, "obs")
    scaled = ((modeled_all - numbers[:, 8:12]) / numbers[:, 12:16]).astype(jnp.bfloat16)
    modeled = lax.dynamic_slice_in_dim(modeled_all, me * block_count, block_count, axis=0)
    coefficient = jnp.where(select, scaled.astype(jnp.float32)[:, :, None, None], 0.0)
    terms = []
    for h in range(hour_count):
        terms.append(
            jnp.sum(feet.astype(jnp.float32) * coefficient[:, None, :, :, h, None], axis=(2, 3))
        )
    terms = jnp.stack(terms, axis=2).reshape(blocks * slot_width, hour_count * chunk)
    high = terms.astype(jnp.bfloat16)
    low = (terms - high.astype(jnp.float32)).astype(jnp.bfloat16)
    spread = onehot.astype(jnp.bfloat16)
    summed = lax.dot_general(
        spread, high, (((0,), (0,)), ((), ())), preferred_element_type=jnp.float32
    ) + lax.dot_general(spread, low, (((0,), (0,)), ((), ())), preferred_element_type=jnp.float32)
    gradient = lax.psum_scatter(
        summed.reshape(total, hour_count, chunk), "flux", scatter_dimension=0, tiled=True
    )
    return (modeled, gradient)


def solution(mesh):
    placed = (
        P(("flux", "obs"), None, None, None, None),
        P(("flux", "obs"), None),
        P(("flux", "obs"), None),
        P(),
        P("flux", None, None),
        P(("flux", "obs"), None),
        P(("flux", "obs"), None),
    )
    return jax.shard_map(
        shards,
        mesh=mesh,
        in_specs=placed,
        out_specs=(P(("flux", "obs"), None), P("flux", None, "obs")),
        check_vma=False,
    )
```

profile of v0, /device:TPU:8, one launch (start us, length us, event | category | flops | bytes accessed | tf_op | source)
XLA Modules:
  0.0 355.8 jit_solution(15153389452616925642)
XLA Ops:
  7.2 3.4 reshape.75
  10.7 2.2 copy.126
  12.8 9.5 %all-to-all-start = ((bf16[32,256,128]{2,1,0:T(8,128)(2,1)}), bf16[32,256,128]{2,1,0:T(8,128)(2,1)S(1)}, u32[]{:S(2)}, u32[]{:S(2)}) async-start(bf16[32,256,128]{2,1,0:T(8,128)(2,1)} %copy.126), calls=%async_computation | async-start | bytes 4194304 | tf_op jit(solution)/shard_map/all_to_all | solution.py:25
  22.8 42.4 %all_gather.6 = f32[256,16]{1,0:T(8,128)S(1)} all-gather(f32[8,16]{1,0:T(8,128)S(1)} %copy.127), channel_id=1, replica_groups=mesh['flux'=16,'obs'=32] {'obs'}, dimensions={0}, use_global_device_ids=true | all-gather | bytes 16896 | tf_op jit(solution)/shard_map/all_gather | solution.py:18
  67.5 1.6 copy.157
  70.1 1.6 copy.158
  73.2 1.6 copy.139
  74.8 1.6 copy.137
  78.3 2.0 broadcast_in_dim.153
  80.3 2.6 broadcast_in_dim.154
  82.9 2.0 broadcast_in_dim.160
  85.0 3.2 broadcast_in_dim.161
  88.2 2.0 broadcast_in_dim.167
  90.2 3.2 broadcast_in_dim.168
  93.5 2.0 broadcast_in_dim.174
  95.5 3.2 broadcast_in_dim.175
  98.7 1.1 broadcast_in_dim.145
  99.9 2.6 broadcast_in_dim.146
  102.5 39.7 %all_gather.7 = bf16[512,5,128]{2,0,1:T(8,128)(2,1)} all-gather(bf16[32,5,128]{2,0,1:T(8,128)(2,1)S(1)} %constant_dynamic-slice_fusion), channel_id=1, replica_groups=mesh['flux'=16,'obs'=32] {'flux'}, dimensions={0}, use_global_device_ids=true | all-gather | bytes 696320 | tf_op jit(solution)/shard_map/all_gather | solution.py:22
  142.3 2.2 copy.131
  144.4 2.2 fusion.4
  146.8 1.1 copy.132
  148.0 1.1 copy.140
  149.1 1.1 copy.138
  150.3 1.2 copy.136
  151.4 1.1 copy.134
  152.5 2.2 broadcast_in_dim.157
  154.8 1.1 broadcast_in_dim.164
  155.9 1.1 broadcast_in_dim.171
  157.0 1.1 broadcast_in_dim.178
  158.1 1.1 broadcast_in_dim.149
  159.2 8.6 %multiply_reduce_fusion.5 = f32[32,256]{1,0:T(8,128)S(1)} fusion(f32[32,256,128]{2,1,0:T(8,128)S(1)} %bitcast.76, f32[32,256,128]{2,1,0:T(8,128)S(1)} %bitcast.75, f32[32,256,128]{2,1,0:T(8,128)S(1)} %bitcast.74, f32[32,256,128]{2,1,0:T(8,128)S(1)} %bitcast.73, f32[32,256,128]{2,1,0:T(8,128)S(1)} %bitcast.77, pred[32,256]{1,0:T(8,128)(4,1)S(1)} %copy-done.7, ...), kind=kLoop, calls=%fused_computation.5 | loop fusion | flops 12574720 | bytes 23142400 | tf_op jit(solution)/shard_map/reduce_sum | solution.py:41
  167.8 4.0 %reduce_sum.72 = f32[256,4,4,2]{3,2,1,0:T(4,128)} reshape(f32[32,256]{1,0:T(8,128)S(1)} %multiply_reduce_fusion.5) | data formatting | bytes 65536 | tf_op jit(solution)/shard_map/reduce_sum | solution.py:41
  171.9 2.1 reduce_sum.73
  174.0 53.2 %psum.7 = f32[256,4]{0,1:T(4,128)S(1)} all-reduce(f32[256,4]{0,1:T(4,128)S(1)} %copy.143), channel_id=1, replica_groups=mesh['flux'=16,'obs'=32] {'obs'}, use_global_device_ids=true, to_apply=%region_3.4 | all-reduce | flops 1024 | bytes 8192 | tf_op jit(solution)/shard_map/psum | solution.py:42
  228.0 1.0 copy.146
  229.0 1.0 copy.150
  230.0 1.0 copy.149
  231.1 1.0 copy.148
  232.1 1.0 copy.147
  233.2 18.6 %multiply_reduce_fusion = (f32[256,4,128]{2,1,0:T(4,128)}, f32[256,4,128]{2,1,0:T(4,128)}, f32[256,4,128]{2,1,0:T(4,128)}, f32[256,4,128]{2,1,0:T(4,128)}, f32[256,4,128]{2,1,0:T(4,128)}) fusion(f32[256,4,2]{2,1,0:T(4,128)} %copy.150, f32[256,4,2]{2,1,0:T(4,128)} %copy.149, f32[256,4,2]{2,1,0:T(4,128)} %copy.148, f32[256,4,2]{2,1,0:T(4,128)} %copy.147, ...), kind=kLoop, calls=%fused_computation | loop fusion | flops 10878976 | bytes 4759552 | tf_op jit(solution)/shard_map/reduce_sum | solution.py:49
  251.8 10.5 %stack.23 = f32[256,4,5,128]{3,2,1,0:T(8,128)} concatenate(f32[256,4,1,128]{3,2,1,0:T(1,128)} %bitcast.86, f32[256,4,1,128]{3,2,1,0:T(1,128)} %bitcast.85, f32[256,4,1,128]{3,2,1,0:T(1,128)} %bitcast.84, f32[256,4,1,128]{3,2,1,0:T(1,128)} %bitcast.83, f32[256,4,1,128]{3,2,1,0:T(1,128)} %bitcast.82), dimensions={2} | concatenate | bytes 5242880 | tf_op jit(solution)/shard_map/stack | solution.py:51
  262.3 3.5 fusion.1
  265.8 4.4 %fusion.6 = f32[512,640]{1,0:T(8,128)} fusion(f32[512,640]{1,0:T(8,128)S(1)} %fusion.1, f32[128,8,5,128]{3,2,1,0:T(8,128)} %bitcast.81, s32[1024]{0:T(1024)S(1)} %copy-done.9), kind=kOutput, calls=%fused_computation.15 | convolution fusion | flops 671940608 | bytes 5246976 | tf_op jit(solution)/shard_map/dot_general | solution.py:55
  270.2 1.7 copy.151
  271.9 1.8 copy.152
  274.4 72.9 %reduce-scatter.2.cloned.1.call-done = f32[32,5,128]{2,1,0:T(8,128)} async-done(((f32[512,5,128]{2,1,0:T(8,128)}), f32[32,5,128]{2,1,0:T(8,128)}) %reduce-scatter.2.cloned.1.call-update) | async-done | bytes 81936 | tf_op jit(solution)/shard_map/reduce_scatter | solution.py:58
  347.4 1.6 copy.153
  (56 shorter events, 8.8 us)
Async XLA Ops:
  7.2 95.3 %copy-start = (bf16[32,5,4096]{2,0,1:T(8,128)(2,1)S(1)}, bf16[32,5,4096]{2,0,1:T(8,128)(2,1)}, u32[]{:S(2)}) copy-start(bf16[32,5,4096]{2,0,1:T(8,128)(2,1)} %param.11) | copy-start | bytes 3932164
  10.6 11.8 %copy-start.12 = (s32[8,4]{0,1:T(4,128)S(1)}, s32[8,4]{0,1:T(4,128)}, u32[]{:S(2)}) copy-start(s32[8,4]{0,1:T(4,128)} %param.8) | copy-start | bytes 388
  10.6 11.8 %copy-start.10 = (s32[512]{0:T(512)S(1)}, s32[512]{0:T(512)}, u32[]{:S(2)}) copy-start(s32[512]{0:T(512)} %param.10) | copy-start | bytes 6148
  10.6 11.8 %copy-start.11 = (s32[8,4]{0,1:T(4,128)S(1)}, s32[8,4]{0,1:T(4,128)}, u32[]{:S(2)}) copy-start(s32[8,4]{0,1:T(4,128)} %param.9) | copy-start | bytes 388
  10.7 12.1 %copy-start.13 = (f32[8,4]{0,1:T(4,128)S(1)}, f32[8,4]{0,1:T(4,128)}, u32[]{:S(2)}) copy-start(f32[8,4]{0,1:T(4,128)} %param.13) | copy-start | bytes 388
  10.7 12.1 %copy-start.14 = (f32[8,4]{0,1:T(4,128)S(1)}, f32[8,4]{0,1:T(4,128)}, u32[]{:S(2)}) copy-start(f32[8,4]{0,1:T(4,128)} %param.12) | copy-start | bytes 388
  12.8 139.7 %all-to-all-start = ((bf16[32,256,128]{2,1,0:T(8,128)(2,1)}), bf16[32,256,128]{2,1,0:T(8,128)(2,1)S(1)}, u32[]{:S(2)}, u32[]{:S(2)}) async-start(bf16[32,256,128]{2,1,0:T(8,128)(2,1)} %copy.126), calls=%async_computation | async-start | bytes 4194304 | tf_op jit(solution)/shard_map/all_to_all | solution.py:25
  22.4 325.0 %reduce-scatter.2.cloned.1.call-start = ((), (), s32[]{:S(2)}) async-start(), calls=%async_computation.2 | async-start | bytes 2228224 | tf_op jit(solution)/shard_map/reduce_scatter | solution.py:58
  152.5 2.2 copy-start.4
  152.5 3.3 copy-start.3
  154.8 2.2 copy-start.2
  155.9 2.2 copy-start.1
  157.0 2.2 copy-start.5
  157.0 2.2 copy-start.6
  157.0 2.2 copy-start.7
  167.8 59.4 %copy-start.8 = (f32[256,4]{0,1:T(4,128)S(1)}, f32[256,4]{0,1:T(4,128)}, u32[]{:S(2)}) copy-start(f32[256,4]{0,1:T(4,128)} %copy.157) | copy-start | bytes 12292
  251.8 10.5 %copy-start.9 = (s32[1024]{0:T(1024)S(1)}, s32[1024]{0:T(1024)}, u32[]{:S(2)}) copy-start(s32[1024]{0:T(1024)} %eq.73) | copy-start | bytes 12292
Sparse Core Ops, SparseCore 0:
  273.9 73.4 reduce-scatter.1
where the time goes:
time: 358 us; the launch traced here: 356 us
  blocking collectives  135 us (38%)
  local copies, waits for them, and re-layouts  82.3 us (23%)
  waiting for transfers between devices  72.9 us (20%)
  other arithmetic  31.1 us (9%)
  between operations  14.4 us (4%)
  matrix products  10.1 us (3%)
  starting transfers between devices  9.58 us (3%)
    reduce_scatter x1, waiting for transfers between devices, shards(): lax.psum_scatter(summed.reshape(total, hour_count, chunk), 'flux', scatte...  72.9 us
    psum x1, blocking collectives, shards(): modeled_all = lax.psum(partial_value, 'obs')  53.2 us
    broadcast_in_dim x27, local copies, waits for them, and re-layouts, shards(): jnp.where(select[:, None, :, :, h, None], windows[:, :, None, None, h, :]...  43.3 us
    all_gather x1, blocking collectives, shards(): numbers = lax.all_gather(numbers, 'obs', axis=0, tiled=True)  42.4 us
    all_gather x1, blocking collectives, shards(): all_flux = lax.all_gather(own_flux, 'flux', axis=0, tiled=True)  39.7 us
    reduce_sum x1, other arithmetic, shards(): jnp.sum(feet.astype(jnp.float32) * coefficient[:, None, :, :, h, None], a...  18.6 us
    reduce_sum x2, other arithmetic, shards(): partial_value = jnp.sum(feet.astype(jnp.float32) * picked, axis=(1, 3, 4))  10.7 us
    another operation x1, local copies, waits for them, and re-layouts, shards(): jnp.stack(terms, axis=2).reshape(blocks * slot_width, hour_count * chunk)  10.5 us
  transfers between devices with their start and end apart: 2, of which 1 were waited for; matrix products, arithmetic and copies ran while one was open for 14% of the time, Pallas kernels for 0%

commit v1 on v0

--- a/solution.py
+++ b/solution.py
@@ -39,7 +39,7 @@
             select[:, None, :, :, h, None], windows[:, :, None, None, h, :], 0.0
         )
     partial_value = jnp.sum(feet.astype(jnp.float32) * picked, axis=(1, 3, 4))
-    modeled_all = lax.psum(partial_value, "obs")
+    modeled_all = jnp.sum(lax.all_gather(partial_value, "obs"), axis=0)
     scaled = ((modeled_all - numbers[:, 8:12]) / numbers[:, 12:16]).astype(jnp.bfloat16)
     modeled = lax.dynamic_slice_in_dim(modeled_all, me * block_count, block_count, axis=0)
     coefficient = jnp.where(select, scaled.astype(jnp.float32)[:, :, None, None], 0.0)

time: 358 us -> 322 us (0.90)
  blocking collectives: 135 us -> 104 us
  waiting for transfers between devices: 72.9 us -> 67.8 us
    psum x1 -> x0, blocking collectives: 53.2 us -> none  [shards(): modeled_all = lax.psum(partial_value, 'obs')]
    all_gather x0 -> x1, blocking collectives: none -> 22.4 us  [shards(): modeled_all = jnp.sum(lax.all_gather(partial_value, 'obs'), axis=0)]
    reduce_scatter x1, waiting for transfers between devices: 72.9 us -> 67.7 us  [shards(): lax.psum_scatter(summed.reshape(total, hour_count, chunk), 'flux', scatte...]
  transfers between devices with their start and end apart: 2 -> 2, of which waited for: 1 -> 1; matrix products, arithmetic and copies ran while one was open for 14% -> 15% of each run, Pallas kernels for 0% -> 0%
where the time goes in v1:
time: 322 us; the launch traced here: 320 us
  blocking collectives  104 us (32%)
  local copies, waits for them, and re-layouts  82.3 us (26%)
  waiting for transfers between devices  67.8 us (21%)
  other arithmetic  31.2 us (10%)
  between operations  14.4 us (4%)
  matrix products  10.1 us (3%)
  starting transfers between devices  9.58 us (3%)
    reduce_scatter x1, waiting for transfers between devices, shards(): lax.psum_scatter(summed.reshape(total, hour_count, chunk), 'flux', scatte...  67.7 us
    broadcast_in_dim x27, local copies, waits for them, and re-layouts, shards(): jnp.where(select[:, None, :, :, h, None], windows[:, :, None, None, h, :]...  43.3 us
    all_gather x1, blocking collectives, shards(): numbers = lax.all_gather(numbers, 'obs', axis=0, tiled=True)  42.4 us
    all_gather x1, blocking collectives, shards(): all_flux = lax.all_gather(own_flux, 'flux', axis=0, tiled=True)  39.7 us
    all_gather x1, blocking collectives, shards(): modeled_all = jnp.sum(lax.all_gather(partial_value, 'obs'), axis=0)  22.4 us
    reduce_sum x1, other arithmetic, shards(): jnp.sum(feet.astype(jnp.float32) * coefficient[:, None, :, :, h, None], a...  18.6 us
    reduce_sum x2, other arithmetic, shards(): partial_value = jnp.sum(feet.astype(jnp.float32) * picked, axis=(1, 3, 4))  10.7 us
    another operation x1, local copies, waits for them, and re-layouts, shards(): jnp.stack(terms, axis=2).reshape(blocks * slot_width, hour_count * chunk)  10.5 us
  transfers between devices with their start and end apart: 2, of which 1 were waited for; matrix products, arithmetic and copies ran while one was open for 15% of the time, Pallas kernels for 0%

profile of v1, /device:TPU:8, one launch (start us, length us, event | category | flops | bytes accessed | tf_op | source)
XLA Modules:
  0.0 319.8 jit_solution(13367567219976026790)
XLA Ops:
  7.2 3.4 %reshape.75 = bf16[256,32,128]{2,1,0:T(8,128)(2,1)S(1)} reshape(bf16[8,4,4,2,4096]{4,3,2,1,0:T(2,128)(2,1)} %param.7) | data formatting | bytes 4194304 | tf_op jit(solution)/shard_map/reshape | solution.py:24
  10.7 2.2 copy.154
  12.8 9.5 %all-to-all-start = ((bf16[32,256,128]{2,1,0:T(8,128)(2,1)}), bf16[32,256,128]{2,1,0:T(8,128)(2,1)S(1)}, u32[]{:S(2)}, u32[]{:S(2)}) async-start(bf16[32,256,128]{2,1,0:T(8,128)(2,1)} %copy.154), calls=%async_computation | async-start | bytes 4194304 | tf_op jit(solution)/shard_map/all_to_all | solution.py:25
  22.8 42.4 %all_gather.12 = f32[256,16]{1,0:T(8,128)S(1)} all-gather(f32[8,16]{1,0:T(8,128)S(1)} %copy.155), channel_id=1, replica_groups=mesh['flux'=16,'obs'=32] {'obs'}, dimensions={0}, use_global_device_ids=true | all-gather | bytes 16896 | tf_op jit(solution)/shard_map/all_gather | solution.py:18
  67.5 1.6 copy.185
  70.1 1.6 copy.186
  73.2 1.6 copy.167
  74.8 1.6 copy.165
  78.3 2.0 broadcast_in_dim.153
  80.3 2.6 broadcast_in_dim.154
  82.9 2.0 broadcast_in_dim.160
  85.0 3.2 %broadcast_in_dim.161 = pred[32,256]{1,0:T(8,128)(4,1)} reshape(pred[256,4,4,2]{3,2,1,0:T(4,128)(4,1)} %broadcast_in_dim.160) | data formatting | bytes 16384 | tf_op jit(solution)/shard_map/jit(_where)/broadcast_in_dim | solution.py:38
  88.2 2.0 broadcast_in_dim.167
  90.2 3.2 %broadcast_in_dim.168 = pred[32,256]{1,0:T(8,128)(4,1)} reshape(pred[256,4,4,2]{3,2,1,0:T(4,128)(4,1)} %broadcast_in_dim.167) | data formatting | bytes 16384 | tf_op jit(solution)/shard_map/jit(_where)/broadcast_in_dim | solution.py:38
  93.5 2.0 broadcast_in_dim.174
  95.5 3.2 %broadcast_in_dim.175 = pred[32,256]{1,0:T(8,128)(4,1)} reshape(pred[256,4,4,2]{3,2,1,0:T(4,128)(4,1)} %broadcast_in_dim.174) | data formatting | bytes 16384 | tf_op jit(solution)/shard_map/jit(_where)/broadcast_in_dim | solution.py:38
  98.7 1.1 broadcast_in_dim.145
  99.9 2.6 broadcast_in_dim.146
  102.5 39.7 %all_gather.13 = bf16[512,5,128]{2,0,1:T(8,128)(2,1)} all-gather(bf16[32,5,128]{2,0,1:T(8,128)(2,1)S(1)} %constant_dynamic-slice_fusion), channel_id=1, replica_groups=mesh['flux'=16,'obs'=32] {'flux'}, dimensions={0}, use_global_device_ids=true | all-gather | bytes 696320 | tf_op jit(solution)/shard_map/all_gather | solution.py:22
  142.3 2.2 copy.159
  144.4 2.2 fusion.4
  146.8 1.1 copy.160
  148.0 1.1 copy.168
  149.1 1.1 copy.166
  150.3 1.2 copy.164
  151.4 1.1 copy.162
  152.5 2.2 broadcast_in_dim.157
  154.8 1.1 broadcast_in_dim.164
  155.9 1.1 broadcast_in_dim.171
  157.0 1.1 broadcast_in_dim.178
  158.1 1.1 broadcast_in_dim.149
  159.2 8.6 %multiply_reduce_fusion.5 = f32[32,256]{1,0:T(8,128)S(1)} fusion(f32[32,256,128]{2,1,0:T(8,128)S(1)} %bitcast.81, f32[32,256,128]{2,1,0:T(8,128)S(1)} %bitcast.80, f32[32,256,128]{2,1,0:T(8,128)S(1)} %bitcast.79, f32[32,256,128]{2,1,0:T(8,128)S(1)} %bitcast.78, f32[32,256,128]{2,1,0:T(8,128)S(1)} %bitcast.82, pred[32,256]{1,0:T(8,128)(4,1)S(1)} %copy-done.7, ...), kind=kLoop, calls=%fused_computation.5 | loop fusion | flops 12574720 | bytes 23142400 | tf_op jit(solution)/shard_map/reduce_sum | solution.py:41
  167.8 4.0 %reduce_sum.81 = f32[256,4,4,2]{3,2,1,0:T(4,128)} reshape(f32[32,256]{1,0:T(8,128)S(1)} %multiply_reduce_fusion.5) | data formatting | bytes 65536 | tf_op jit(solution)/shard_map/reduce_sum | solution.py:41
  171.9 2.1 reduce_sum.82
  174.0 22.4 %all-gather = f32[8192,4]{0,1:T(4,128)S(1)} all-gather(f32[256,4]{0,1:T(4,128)S(1)} %copy.171), channel_id=2, replica_groups=mesh['flux'=16,'obs'=32] {'obs'}, dimensions={0}, use_global_device_ids=true | all-gather | bytes 135168 | tf_op jit(solution)/shard_map/all_gather | solution.py:42
  197.2 1.0 copy.174
  198.2 1.0 copy.178
  199.2 1.0 copy.177
  200.3 1.0 copy.176
  201.3 1.0 copy.175
  202.4 18.6 %multiply_reduce_fusion = (f32[256,4,128]{2,1,0:T(4,128)}, f32[256,4,128]{2,1,0:T(4,128)}, f32[256,4,128]{2,1,0:T(4,128)}, f32[256,4,128]{2,1,0:T(4,128)}, f32[256,4,128]{2,1,0:T(4,128)}) fusion(f32[256,4,2]{2,1,0:T(4,128)} %copy.178, f32[256,4,2]{2,1,0:T(4,128)} %copy.177, f32[256,4,2]{2,1,0:T(4,128)} %copy.176, f32[256,4,2]{2,1,0:T(4,128)} %copy.175, ...), kind=kLoop, calls=%fused_computation | loop fusion | flops 10878976 | bytes 4759552 | tf_op jit(solution)/shard_map/reduce_sum | solution.py:49
  221.0 10.5 %stack.23 = f32[256,4,5,128]{3,2,1,0:T(8,128)} concatenate(f32[256,4,1,128]{3,2,1,0:T(1,128)} %bitcast.91, f32[256,4,1,128]{3,2,1,0:T(1,128)} %bitcast.90, f32[256,4,1,128]{3,2,1,0:T(1,128)} %bitcast.89, f32[256,4,1,128]{3,2,1,0:T(1,128)} %bitcast.88, f32[256,4,1,128]{3,2,1,0:T(1,128)} %bitcast.87), dimensions={2} | concatenate | bytes 5242880 | tf_op jit(solution)/shard_map/stack | solution.py:51
  231.5 3.5 %fusion.1 = f32[512,640]{1,0:T(8,128)S(1)} fusion(f32[128,8,5,128]{3,2,1,0:T(8,128)} %bitcast.85, s32[1024]{0:T(1024)S(1)} %copy-done.9), kind=kOutput, calls=%fused_computation.10 | convolution fusion | flops 674234368 | bytes 3936256 | tf_op jit(solution)/shard_map/dot_general | solution.py:57
  235.0 4.4 %fusion.6 = f32[512,640]{1,0:T(8,128)} fusion(f32[512,640]{1,0:T(8,128)S(1)} %fusion.1, f32[128,8,5,128]{3,2,1,0:T(8,128)} %bitcast.86, s32[1024]{0:T(1024)S(1)} %copy-done.9), kind=kOutput, calls=%fused_computation.15 | convolution fusion | flops 671940608 | bytes 5246976 | tf_op jit(solution)/shard_map/dot_general | solution.py:55
  239.4 1.7 copy.179
  241.1 1.8 copy.180
  243.6 67.7 %reduce-scatter.2.cloned.1.call-done = f32[32,5,128]{2,1,0:T(8,128)} async-done(((f32[512,5,128]{2,1,0:T(8,128)}), f32[32,5,128]{2,1,0:T(8,128)}) %reduce-scatter.2.cloned.1.call-update) | async-done | bytes 81936 | tf_op jit(solution)/shard_map/reduce_scatter | solution.py:58
  311.4 1.6 copy.181
  (57 shorter events, 8.8 us)
Async XLA Ops:
  7.2 95.3 %copy-start = (bf16[32,5,4096]{2,0,1:T(8,128)(2,1)S(1)}, bf16[32,5,4096]{2,0,1:T(8,128)(2,1)}, u32[]{:S(2)}) copy-start(bf16[32,5,4096]{2,0,1:T(8,128)(2,1)} %param.11) | copy-start | bytes 3932164
  10.6 11.8 %copy-start.12 = (s32[8,4]{0,1:T(4,128)S(1)}, s32[8,4]{0,1:T(4,128)}, u32[]{:S(2)}) copy-start(s32[8,4]{0,1:T(4,128)} %param.8) | copy-start | bytes 388
  10.6 11.8 %copy-start.10 = (s32[512]{0:T(512)S(1)}, s32[512]{0:T(512)}, u32[]{:S(2)}) copy-start(s32[512]{0:T(512)} %param.10) | copy-start | bytes 6148
  10.6 11.8 %copy-start.11 = (s32[8,4]{0,1:T(4,128)S(1)}, s32[8,4]{0,1:T(4,128)}, u32[]{:S(2)}) copy-start(s32[8,4]{0,1:T(4,128)} %param.9) | copy-start | bytes 388
  10.7 12.1 %copy-start.13 = (f32[8,4]{0,1:T(4,128)S(1)}, f32[8,4]{0,1:T(4,128)}, u32[]{:S(2)}) copy-start(f32[8,4]{0,1:T(4,128)} %param.13) | copy-start | bytes 388
  10.7 12.1 %copy-start.14 = (f32[8,4]{0,1:T(4,128)S(1)}, f32[8,4]{0,1:T(4,128)}, u32[]{:S(2)}) copy-start(f32[8,4]{0,1:T(4,128)} %param.12) | copy-start | bytes 388
  12.8 139.7 %all-to-all-start = ((bf16[32,256,128]{2,1,0:T(8,128)(2,1)}), bf16[32,256,128]{2,1,0:T(8,128)(2,1)S(1)}, u32[]{:S(2)}, u32[]{:S(2)}) async-start(bf16[32,256,128]{2,1,0:T(8,128)(2,1)} %copy.154), calls=%async_computation | async-start | bytes 4194304 | tf_op jit(solution)/shard_map/all_to_all | solution.py:25
  22.4 289.0 %reduce-scatter.2.cloned.1.call-start = ((), (), s32[]{:S(2)}) async-start(), calls=%async_computation.2 | async-start | bytes 2228224 | tf_op jit(solution)/shard_map/reduce_scatter | solution.py:58
  152.5 2.2 copy-start.4
  152.5 3.3 %copy-start.3 = (f32[256,4,128]{2,1,0:T(4,128)S(1)}, f32[256,4,128]{2,1,0:T(4,128)}, u32[]{:S(2)}) copy-start(f32[256,4,128]{2,1,0:T(4,128)} %copy.166) | copy-start | bytes 1572868
  154.8 2.2 copy-start.2
  155.9 2.2 copy-start.1
  157.0 2.2 copy-start.5
  157.0 2.2 copy-start.6
  157.0 2.2 copy-start.7
  167.8 28.6 %copy-start.8 = (f32[256,4]{0,1:T(4,128)S(1)}, f32[256,4]{0,1:T(4,128)}, u32[]{:S(2)}) copy-start(f32[256,4]{0,1:T(4,128)} %copy.185) | copy-start | bytes 12292
  221.0 10.5 %copy-start.9 = (s32[1024]{0:T(1024)S(1)}, s32[1024]{0:T(1024)}, u32[]{:S(2)}) copy-start(s32[1024]{0:T(1024)} %eq.73) | copy-start | bytes 12292
Sparse Core Ops, SparseCore 0:
  243.1 68.2 reduce-scatter.1
